TPU v7x, 256 devices: a whole 4x4x8 slice. The times are simulated.
256 devices in a mesh: dp: 32 (over y_lo, z, core), tensor: 8 (over y_hi, x).
Axes of the slice: x: 4, y: 4 (y_hi: 2, y_lo: 2; y = y_hi * 2 + y_lo), z: 8, core: 2. Of those that a mesh axis runs over, the one named last changes fastest.
Arguments:
- activations: bfloat16 [1024, 16384], P('dp', 'tensor'), may hold values from -6 to 6
- weight: bfloat16 [16384, 16384], P('tensor', 'dp'), may hold values from -0.046875 to 0.046875
- out_grad: bfloat16 [1024, 16384], P('tensor', 'dp'), may hold values from -6 to 6
Outputs:
- outputs: bfloat16 [1024, 16384], P('tensor', 'dp')
- in_grad: bfloat16 [1024, 16384], P('dp', 'tensor')
- weight_grad: float32 [16384, 16384], P('tensor', 'dp')
All inputs are finite; a program needn't handle non-finite values.
Results may differ from a plain program's by a relative error of at most 0.0049.
Values may be sent and summed in bfloat16 or wider, within the bound.
A program may use at most 64 MiB of HBM per device.

v0:
```python
import math

import jax
import jax.numpy as jnp
from jax import lax
from jax.sharding import PartitionSpec as P


def from_partner(shard, axis, apart):
    return lax.ppermute(shard, axis, [(i, i ^ 1 << apart) for i in range(lax.axis_size(axis))])


def signs_table(width):
    position = jnp.arange(width, dtype=jnp.int32)
    joined = jnp.bitwise_and(position[:, None], position[None, :])
    parity = jnp.zeros_like(joined)
    for bit_number in range(width.bit_length() - 1):
        parity = parity + jnp.bitwise_and(jnp.right_shift(joined, bit_number), 1)
    return jnp.where(parity % 2 == 1, -1.0, 1.0).astype(jnp.float32)


def transform(values, width):
    bit_count = width.bit_length() - 1
    first_size = 2 ** (bit_count // 2)
    second = width // first_size
    shaped = values.reshape(values.shape[0], first_size, second)
    result = jnp.einsum(
        "rab,ac->rcb", shaped, signs_table(first_size), precision=lax.Precision.HIGHEST
    )
    result = jnp.einsum("rcb,bd->rcd", result, signs_table(second), precision=lax.Precision.HIGHEST)
    return result.reshape(values.shape[0], width)


def rotate_pairs(values, width):
    result = transform(values, width)
    position = lax.axis_index("tensor")
    for bit_number in range(lax.axis_size("tensor").bit_length() - 1):
        other = from_partner(result, "tensor", bit_number)
        upper = jnp.bitwise_and(jnp.right_shift(position, bit_number), 1) == 1
        result = jnp.where(upper, other - result, result + other)
    return result


def per_device(activations, weight, out_grad):
    tensor_size = lax.axis_size("tensor")
    local_width = activations.shape[1]
    full_width = local_width * tensor_size
    factor = 1.0 / math.sqrt(full_width)
    grad_count = out_grad.shape[0]
    token_total = grad_count * tensor_size
    rotated = (rotate_pairs(activations.astype(jnp.float32), local_width) * factor).astype(
        jnp.bfloat16
    )
    grad_all = lax.all_gather(out_grad, "tensor", axis=0, tiled=True)
    rows_all = lax.all_gather(rotated, "dp", axis=0, tiled=True)
    weight_grad = lax.dot_general(
        rows_all, grad_all, (((0,), (0,)), ((), ())), preferred_element_type=jnp.float32
    )
    outputs = lax.psum_scatter(
        jnp.dot(rows_all, weight, preferred_element_type=jnp.float32),
        "tensor",
        scatter_dimension=0,
        tiled=True,
    ).astype(jnp.bfloat16)
    weight_grad = weight_grad * (1.0 / math.sqrt(token_total))
    rotated_grad = lax.psum_scatter(
        lax.dot_general(
            grad_all, weight, (((1,), (1,)), ((), ())), preferred_element_type=jnp.float32
        ),
        "dp",
        scatter_dimension=0,
        tiled=True,
    )
    in_grad = (rotate_pairs(rotated_grad, local_width) * factor).astype(jnp.bfloat16)
    return (outputs, in_grad, weight_grad)


def solution(mesh):
    return jax.shard_map(
        per_device,
        mesh=mesh,
        in_specs=(P("dp", "tensor"), P("tensor", "dp"), P("tensor", "dp")),
        out_specs=(P("tensor", "dp"), P("dp", "tensor"), P("tensor", "dp")),
        check_vma=False,
    )
```

profile of v0, /device:TPU:1, one launch (start us, length us, event | category | flops | bytes accessed | tf_op | source)
XLA Modules:
  0.0 355.9 jit_solution(6116350609848868271)
XLA Ops:
  7.2 0.0 copy-start
  7.2 0.0 all-gather.5.cloned.1.call-start
  7.2 1.3 reshape.18
  8.5 0.4 convolution_bitcast_fusion.1
  9.0 0.6 fusion.4
  9.6 0.2 reshape.19
  9.8 2.1 collective-permute-start
  11.9 0.0 all-gather.5.cloned.1.call-update
  11.9 0.0 all-gather.3.cloned.1.call-start
  12.0 4.6 %collective-permute-done = f32[32,2048]{1,0:T(8,128)S(1)} collective-permute-done((f32[32,2048]{1,0:T(8,128)S(1)}, f32[32,2048]{1,0:T(8,128)S(1)}, u32[]{:S(2)}, u32[]{:S(2)}) %collective-permute-start) | collective-permute-done | bytes 262176 | tf_op jit(solution)/shard_map/ppermute | solution.py:10
  16.6 4.1 %collective-permute-start.1 = (f32[32,2048]{1,0:T(8,128)S(1)}, f32[32,2048]{1,0:T(8,128)S(1)}, u32[]{:S(2)}, u32[]{:S(2)}) collective-permute-start(f32[32,2048]{1,0:T(8,128)S(1)} %add_select_fusion.3), channel_id=1, source_target_pairs={{0,2},{1,3},{2,0},{3,1},{4,6},{5,7},{6,4},{7,5},{8,10},{9,11},{10,... | collective-permute-start | bytes 786440 | tf_op jit(solution)/shard_map/ppermute | solution.py:10
  20.7 4.5 %collective-permute-done.1 = f32[32,2048]{1,0:T(8,128)S(1)} collective-permute-done((f32[32,2048]{1,0:T(8,128)S(1)}, f32[32,2048]{1,0:T(8,128)S(1)}, u32[]{:S(2)}, u32[]{:S(2)}) %collective-permute-start.1) | collective-permute-done | bytes 262176 | tf_op jit(solution)/shard_map/ppermute | solution.py:10
  25.3 3.5 collective-permute-start.2
  28.8 6.2 %collective-permute-done.2 = f32[32,2048]{1,0:T(8,128)S(1)} collective-permute-done((f32[32,2048]{1,0:T(8,128)S(1)}, f32[32,2048]{1,0:T(8,128)S(1)}, u32[]{:S(2)}, u32[]{:S(2)}) %collective-permute-start.2) | collective-permute-done | bytes 262176 | tf_op jit(solution)/shard_map/ppermute | solution.py:10
  35.0 0.7 multiply_convert_fusion.1
  35.7 0.0 all-gather.3.cloned.1.call-update
  35.7 0.0 reduce-scatter.5.cloned.1.call-start
  35.8 30.8 %all-gather.5.cloned.1.call-done = bf16[1024,512]{1,0:T(8,128)(2,1)} async-done(((bf16[128,512]{1,0:T(8,128)(2,1)}), bf16[1024,512]{1,0:T(8,128)(2,1)}) %all-gather.5.cloned.1.call-update) | async-done | bytes 1048592 | tf_op jit(solution)/shard_map/all_gather | solution.py:54
  66.6 0.0 copy-done
  66.6 6.8 %fusion.57 = f32[1024,2048]{1,0:T(8,128)} fusion(bf16[1024,512]{1,0:T(8,128)(2,1)} %all-gather.5.cloned.1.call-done, bf16[2048,512]{1,0:T(8,128)(2,1)S(1)} %copy-done), kind=kOutput, calls=%fused_computation.68 | convolution fusion | flops 2147483648 | bytes 11534336 | tf_op jit(solution)/shard_map/dot_general | solution.py:67
  73.4 0.0 reduce-scatter.5.cloned.1.call-update
  73.5 0.0 reduce-scatter.3.cloned.1.call-start
  73.5 62.6 %all-gather.3.cloned.1.call-done = bf16[1024,2048]{1,0:T(8,128)(2,1)} async-done(((bf16[32,2048]{1,0:T(8,128)(2,1)}), bf16[1024,2048]{1,0:T(8,128)(2,1)}) %all-gather.3.cloned.1.call-update) | async-done | bytes 4194320 | tf_op jit(solution)/shard_map/all_gather | solution.py:55
  136.1 5.9 %fusion.56 = f32[1024,512]{1,0:T(8,128)} fusion(bf16[1024,2048]{1,0:T(8,128)(2,1)} %all-gather.3.cloned.1.call-done, bf16[2048,512]{1,0:T(8,128)(2,1)S(1)} %copy-done), kind=kOutput, calls=%fused_computation.67 | convolution fusion | flops 2147483648 | bytes 8388608 | tf_op jit(solution)/shard_map/dot_general | solution.py:60
  142.0 0.0 reduce-scatter.3.cloned.1.call-update
  142.0 120.9 %reduce-scatter.5.cloned.1.call-done = f32[32,2048]{1,0:T(8,128)} async-done(((f32[1024,2048]{1,0:T(8,128)}), f32[32,2048]{1,0:T(8,128)}) %reduce-scatter.5.cloned.1.call-update) | async-done | bytes 262160 | tf_op jit(solution)/shard_map/reduce_scatter | solution.py:66
  262.9 1.1 reshape.20
  264.0 0.6 convolution_bitcast_fusion
  264.7 0.6 fusion.2
  265.3 0.2 reshape.21
  265.5 1.6 collective-permute-start.3
  267.1 3.8 %collective-permute-done.3 = f32[32,2048]{1,0:T(8,128)S(1)} collective-permute-done((f32[32,2048]{1,0:T(8,128)S(1)}, f32[32,2048]{1,0:T(8,128)S(1)}, u32[]{:S(2)}, u32[]{:S(2)}) %collective-permute-start.3) | collective-permute-done | bytes 262176 | tf_op jit(solution)/shard_map/ppermute | solution.py:10
  270.9 2.7 collective-permute-start.4
  273.5 6.7 %collective-permute-done.4 = f32[32,2048]{1,0:T(8,128)S(1)} collective-permute-done((f32[32,2048]{1,0:T(8,128)S(1)}, f32[32,2048]{1,0:T(8,128)S(1)}, u32[]{:S(2)}, u32[]{:S(2)}) %collective-permute-start.4) | collective-permute-done | bytes 262176 | tf_op jit(solution)/shard_map/ppermute | solution.py:10
  280.3 2.7 collective-permute-start.5
  283.0 6.9 %convolution_multiply_fusion = f32[2048,512]{1,0:T(8,128)} fusion(bf16[1024,2048]{1,0:T(8,128)(2,1)} %all-gather.3.cloned.1.call-done, bf16[1024,512]{1,0:T(8,128)(2,1)} %all-gather.5.cloned.1.call-done), kind=kOutput, calls=%fused_computation | convolution fusion | flops 2148532224 | bytes 9437184 | tf_op jit(solution)/shard_map/dot_general | solution.py:56
  289.9 57.2 %reduce-scatter.3.cloned.1.call-done = f32[128,512]{1,0:T(8,128)} async-done(((f32[1024,512]{1,0:T(8,128)}), f32[128,512]{1,0:T(8,128)}) %reduce-scatter.3.cloned.1.call-update) | async-done | bytes 262160 | tf_op jit(solution)/shard_map/reduce_scatter | solution.py:59
  347.1 1.6 convert_element_type.11
  348.7 0.0 collective-permute-done.5
  348.7 0.7 multiply_convert_fusion
  (4 shorter events, 0.1 us)
Async XLA Ops:
  7.2 59.5 %copy-start = (bf16[2048,512]{1,0:T(8,128)(2,1)S(1)}, bf16[2048,512]{1,0:T(8,128)(2,1)}, u32[]{:S(2)}) copy-start(bf16[2048,512]{1,0:T(8,128)(2,1)} %param.4) | copy-start | bytes 6291460
  7.2 59.4 %all-gather.5.cloned.1.call-start = ((), (), s32[]{:S(2)}) async-start(), calls=%async_computation.4 | async-start | bytes 1179648 | tf_op jit(solution)/shard_map/all_gather | solution.py:54
  9.8 6.8 %collective-permute-start = (f32[32,2048]{1,0:T(8,128)S(1)}, f32[32,2048]{1,0:T(8,128)S(1)}, u32[]{:S(2)}, u32[]{:S(2)}) collective-permute-start(f32[32,2048]{1,0:T(8,128)S(1)} %reshape.19), channel_id=1, source_target_pairs={{0,1},{1,0},{2,3},{3,2},{4,5},{5,4},{6,7},{7,6},{8,9},{9,8},{10,11... | collective-permute-start | bytes 786440 | tf_op jit(solution)/shard_map/ppermute | solution.py:10
  11.9 124.2 %all-gather.3.cloned.1.call-start = ((), (), s32[]{:S(2)}) async-start(), calls=%async_computation.2 | async-start | bytes 4325376 | tf_op jit(solution)/shard_map/all_gather | solution.py:55
  16.6 8.6 %collective-permute-start.1 = (f32[32,2048]{1,0:T(8,128)S(1)}, f32[32,2048]{1,0:T(8,128)S(1)}, u32[]{:S(2)}, u32[]{:S(2)}) collective-permute-start(f32[32,2048]{1,0:T(8,128)S(1)} %add_select_fusion.3), channel_id=1, source_target_pairs={{0,2},{1,3},{2,0},{3,1},{4,6},{5,7},{6,4},{7,5},{8,10},{9,11},{10,... | collective-permute-start | bytes 786440 | tf_op jit(solution)/shard_map/ppermute | solution.py:10
  25.3 9.7 %collective-permute-start.2 = (f32[32,2048]{1,0:T(8,128)S(1)}, f32[32,2048]{1,0:T(8,128)S(1)}, u32[]{:S(2)}, u32[]{:S(2)}) collective-permute-start(f32[32,2048]{1,0:T(8,128)S(1)} %add_select_fusion.2), channel_id=1, source_target_pairs={{0,4},{1,5},{2,6},{3,7},{4,0},{5,1},{6,2},{7,3},{8,12},{9,13},{10,... | collective-permute-start | bytes 786440 | tf_op jit(solution)/shard_map/ppermute | solution.py:10
  35.7 227.1 %reduce-scatter.5.cloned.1.call-start = ((), (), s32[]{:S(2)}) async-start(), calls=%async_computation.5 | async-start | bytes 8650752 | tf_op jit(solution)/shard_map/reduce_scatter | solution.py:66
  73.5 273.6 %reduce-scatter.3.cloned.1.call-start = ((), (), s32[]{:S(2)}) async-start(), calls=%async_computation.3 | async-start | bytes 2359296 | tf_op jit(solution)/shard_map/reduce_scatter | solution.py:59
  265.5 5.4 %collective-permute-start.3 = (f32[32,2048]{1,0:T(8,128)S(1)}, f32[32,2048]{1,0:T(8,128)S(1)}, u32[]{:S(2)}, u32[]{:S(2)}) collective-permute-start(f32[32,2048]{1,0:T(8,128)S(1)} %reshape.21), channel_id=1, source_target_pairs={{0,1},{1,0},{2,3},{3,2},{4,5},{5,4},{6,7},{7,6},{8,9},{9,8},{10,11... | collective-permute-start | bytes 786440 | tf_op jit(solution)/shard_map/ppermute | solution.py:10
  270.9 9.4 %collective-permute-start.4 = (f32[32,2048]{1,0:T(8,128)S(1)}, f32[32,2048]{1,0:T(8,128)S(1)}, u32[]{:S(2)}, u32[]{:S(2)}) collective-permute-start(f32[32,2048]{1,0:T(8,128)S(1)} %add_select_fusion.1), channel_id=1, source_target_pairs={{0,2},{1,3},{2,0},{3,1},{4,6},{5,7},{6,4},{7,5},{8,10},{9,11},{10,... | collective-permute-start | bytes 786440 | tf_op jit(solution)/shard_map/ppermute | solution.py:10
  280.3 68.4 %collective-permute-start.5 = (f32[32,2048]{1,0:T(8,128)S(1)}, f32[32,2048]{1,0:T(8,128)S(1)}, u32[]{:S(2)}, u32[]{:S(2)}) collective-permute-start(f32[32,2048]{1,0:T(8,128)S(1)} %add_select_fusion), channel_id=1, source_target_pairs={{0,4},{1,5},{2,6},{3,7},{4,0},{5,1},{6,2},{7,3},{8,12},{9,13},{10,... | collective-permute-start | bytes 786440 | tf_op jit(solution)/shard_map/ppermute | solution.py:10
Sparse Core Ops, SparseCore 0:
  12.0 54.5 all-gather.4
  69.0 67.0 all-gather.2
  138.7 124.1 reduce-scatter.4
  266.8 80.2 reduce-scatter.2
where the time goes:
time: 357 us; the launch traced here: 356 us
  waiting for transfers between devices  297 us (83%)
  matrix products  21.8 us (6%)
  starting transfers between devices  16.9 us (5%)
  between operations  13.8 us (4%)
    reduce_scatter x1, waiting for transfers between devices, per_device(): lax.psum_scatter(lax.dot_general(grad_all, weight, (((1,), (1,)), ((), ()...  121 us
    all_gather x1, waiting for transfers between devices, per_device(): rows_all = lax.all_gather(rotated, 'dp', axis=0, tiled=True)  62.6 us
    reduce_scatter x1, waiting for transfers between devices, per_device(): lax.psum_scatter(jnp.dot(rows_all, weight, preferred_element_type=jnp.flo...  57.2 us
    all_gather x1, waiting for transfers between devices, per_device(): grad_all = lax.all_gather(out_grad, 'tensor', axis=0, tiled=True)  30.8 us
    ppermute x6, waiting for transfers between devices, from_partner(): lax.ppermute(shard, axis, [(i, i ^ 1 << apart) for i in range(lax.axis_si...  25.8 us
    ppermute x6, starting transfers between devices, from_partner(): lax.ppermute(shard, axis, [(i, i ^ 1 << apart) for i in range(lax.axis_si...  16.7 us
  transfers between devices with their start and end apart: 10, of which 9 were waited for; matrix products, arithmetic and copies ran while one was open for 7% of the time, Pallas kernels for 0%

commit v1 on v0

v1 whole, which is shorter than its diff:
```python
import functools
import math

import jax
import jax.numpy as jnp
import numpy as np
from jax import lax
from jax.experimental import pallas as pl
from jax.experimental.pallas import tpu as pltpu
from jax.sharding import PartitionSpec as P

MESH = pl.DeviceIdType.MESH
YL, Z, C, T = 2, 8, 2, 8
F32, BF16 = jnp.float32, jnp.bfloat16
SEMS = 256


def signs_table(width):
    position = np.arange(width)
    joined = position[:, None] & position[None, :]
    parity = np.zeros_like(joined)
    for bit_number in range(width.bit_length() - 1):
        parity = parity + ((joined >> bit_number) & 1)
    return np.where(parity % 2 == 1, -1.0, 1.0)


def butterfly(parts):
    parts = list(parts)
    apart = 1
    while apart < len(parts):
        for low in range(len(parts)):
            if low & apart == 0:
                a, b = parts[low], parts[low | apart]
                parts[low], parts[low | apart] = a + b, a - b
        apart *= 2
    return parts


def kernel(scale, grad_scale, act, w, og, had, out, ing, wg, w2, s1, x1, s2, r, g, g2, pf,
           sbp, sbm, rp, rm, ys, yr, q, xq, t1, v1, t2, igb, wgv, rg, sems, local_sems):
    d, t = lax.axis_index("dp"), lax.axis_index("tensor")
    c, z, yl = d % C, (d // C) % Z, d // (C * Z)
    tokens, width = act.shape
    chunk = width // T

    def block(rel, zz, core):
        return (((yl + rel) % YL) * Z + (zz + 2 * Z) % Z) * C + core

    sib = (block(0, z, 1 - c), t)
    zp, zm = (block(0, z + 1, c), t), (block(0, z - 1, c), t)
    yp = (block(1, z, c), t)
    peers = [(d, (t + j) % T) for j in range(1, T)]

    barrier = pltpu.get_barrier_semaphore()
    everyone = [sib, zp, zm, yp] + peers
    for other in everyone:
        pl.semaphore_signal(barrier, inc=1, device_id=other, device_id_type=MESH)
    pl.semaphore_wait(barrier, len(everyone))

    used = [0]
    sent = []

    def pair():
        used[0] += 2
        return used[0] - 2

    def remote(src, dst, to, number):
        return pltpu.make_async_remote_copy(
            src_ref=src, dst_ref=dst, send_sem=sems.at[number], recv_sem=sems.at[number + 1],
            device_id=to, device_id_type=MESH)

    def send(src, dst, to, number):
        copy = remote(src, dst, to, number)
        copy.start()
        sent.append(copy)

    def arrive(dst, number):
        remote(dst, dst, sib, number).wait_recv()

    def local_rotation(parts):
        rows = jnp.concatenate(parts, axis=0)
        table = had[...]
        if rows.dtype == BF16:
            mixed = jnp.dot(rows, table, preferred_element_type=F32)
        else:
            high = rows.astype(BF16)
            rest = rows - high.astype(F32)
            middle = rest.astype(BF16)
            low = (rest - middle.astype(F32)).astype(BF16)
            mixed = (jnp.dot(high, table, preferred_element_type=F32)
                     + jnp.dot(middle, table, preferred_element_type=F32)
                     + jnp.dot(low, table, preferred_element_type=F32))
        return butterfly([mixed[k * tokens:(k + 1) * tokens] for k in range(T)])

    def rotate(parts, first, first_in, second, landing):
        for k, part in enumerate(local_rotation(parts)):
            first[k] = part
        numbers = [pair() for _ in peers]
        for j, peer in enumerate(peers):
            send(first.at[peer[1]], first_in.at[t], peer, numbers[j])
        first_in[t] = first[t]
        for j in range(1, T):
            arrive(first_in.at[(t + T - j) % T], numbers[j - 1])
        for k, part in enumerate(butterfly([first_in[k] for k in range(T)])):
            second[k] = (part * scale).astype(BF16)
        numbers = [pair() for _ in peers]
        for j, peer in enumerate(peers):
            send(second.at[peer[1]], landing.at[t], peer, numbers[j])
        landing[t] = second[t]

        def finish():
            for j in range(1, T):
                arrive(landing.at[(t + T - j) % T], numbers[j - 1])

        return finish

    w_number = pair()
    send(w, w2, sib, w_number)

    own = block(0, z, c)
    finish = rotate([act[:, k * chunk:(k + 1) * chunk] for k in range(T)], s1, x1, s2, r.at[own])

    gather_numbers = [pair() for _ in peers]
    for j, peer in enumerate(peers):
        send(og, g.at[pl.ds(2 * t, 2)], peer, gather_numbers[j])
    g[pl.ds(2 * t, 2)] = og[...]

    finish()

    to_sib = []

    def share(rel, zz):
        number = pair()
        send(r.at[block(rel, zz, c)], r.at[block(rel, zz, c)], sib, number)
        to_sib.append((block(rel, zz, 1 - c), number))

    numbers = {(sign, rel, s): pair() for sign in (1, -1) for rel in (0, 1) for s in range(4)}

    def pass_on(sign, rel, zz, s):
        b = block(rel, zz, c)
        send(r.at[b], r.at[b], zp if sign == 1 else zm, numbers[sign, rel, s])

    y_number = pair()
    send(r.at[own], r.at[own], yp, y_number)
    pass_on(1, 0, z, 0)
    pass_on(-1, 0, z, 0)
    share(0, z)
    arrive(r.at[block(1, z, c)], y_number)
    pass_on(1, 1, z, 0)
    pass_on(-1, 1, z, 0)
    share(1, z)

    def ring_step(s):
        for rel in (0, 1):
            for sign in (1, -1):
                keep = 0 if sign == 1 else 1
                if s == 3 and rel != keep:
                    continue
                zz = z - sign * (1 + s)
                arrive(r.at[block(rel, zz, c)], numbers[sign, rel, s])
                if s < 2 or (s == 2 and rel == keep):
                    pass_on(sign, rel, zz, s + 1)
                share(rel, zz)

    ring_step(0)
    for j in range(1, T):
        arrive(g.at[pl.ds(2 * ((t + T - j) % T), 2)], gather_numbers[j - 1])
    g2_number = pair()
    send(g.at[:, 1 - c], g2, sib, g2_number)
    ring_step(1)
    arrive(g2, g2_number)
    arrive(w2, w_number)

    rows = Z * YL * tokens

    def partial(k, carry):
        mine = g[:, c].reshape(rows, g.shape[-1])
        theirs = g2[...].reshape(rows, g.shape[-1])
        at = pl.ds(pl.multiple_of(k * chunk, chunk), chunk)
        dims = (((1,), (1,)), ((), ()))
        total = (lax.dot_general(mine, w[at, :], dims, preferred_element_type=F32)
                 + lax.dot_general(theirs, w2[at, :], dims, preferred_element_type=F32))
        pf[:, k] = total.reshape(Z * YL, tokens, chunk)
        return carry

    lax.fori_loop(0, T, partial, 0)
    ring_step(2)

    sums = {(sign, rel, s): pair() for sign in (1, -1) for rel in (0, 1) for s in range(4)}

    def reduce_step(s):
        for rel in (0, 1):
            for sign in (1, -1):
                keep = 0 if sign == 1 else 1
                if s == 0 and rel != keep:
                    continue
                into, out_of, to = (rp, sbp, zp) if sign == 1 else (rm, sbm, zm)
                target = block(rel, z + sign * (4 - s), 0) // C
                total = pf[target]
                if s > 1 or (s == 1 and rel == keep):
                    arrive(into.at[rel, s - 1], sums[sign, rel, s - 1])
                    total = total + into[rel, s - 1].astype(F32)
                out_of[rel, s] = total.astype(BF16)
                send(out_of.at[rel, s], into.at[rel, s], to, sums[sign, rel, s])

    reduce_step(0)
    ring_step(3)
    for b, number in to_sib:
        arrive(r.at[b], number)

    def products(i, carry):
        total = jnp.zeros((256, w.shape[1]), F32)
        for k in range(T):
            lhs = r[pl.ds(8 * i, 8), k].reshape(256, chunk)
            total = total + jnp.dot(lhs, w[k * chunk:(k + 1) * chunk, :], preferred_element_type=F32)
        q[pl.ds(2 * i, 2)] = total.reshape(2, 128, w.shape[1]).astype(BF16)
        return carry

    lax.fori_loop(0, 4, products, 0)
    out_numbers = [pair() for _ in peers]
    for j, peer in enumerate(peers):
        send(q.at[peer[1]], xq.at[t], peer, out_numbers[j])
    xq[t] = q[t]

    def weight_grad(k, carry):
        lhs = r[:, k].reshape(2 * rows, chunk)
        rhs = g[...].reshape(2 * rows, g.shape[-1])
        total = lax.dot_general(lhs, rhs, (((0,), (0,)), ((), ())), preferred_element_type=F32)
        at = pl.ds(pl.multiple_of(k * chunk, chunk), chunk)
        wgv[at, :] = total * grad_scale
        pltpu.make_async_copy(wgv.at[at, :], wg.at[at, :], local_sems.at[k]).start()
        return carry

    reduce_step(1)
    lax.fori_loop(0, 3, weight_grad, 0)
    reduce_step(2)
    lax.fori_loop(3, 6, weight_grad, 0)
    reduce_step(3)
    lax.fori_loop(6, 8, weight_grad, 0)

    finals = []
    for rel in (1, 0):
        total = pf[block(rel, z, 0) // C]
        for sign, into in ((1, rp), (-1, rm)):
            arrive(into.at[rel, 3], sums[sign, rel, 3])
            total = total + into[rel, 3].astype(F32)
        if rel == 1:
            ys[...] = total.astype(BF16)
            back_number = pair()
            send(ys, yr, yp, back_number)
        else:
            rg[...] = total
    arrive(yr, back_number)
    finish = rotate([rg[k] + yr[k].astype(F32) for k in range(T)], t1, v1, t2, igb)

    for j in range(1, T):
        arrive(xq.at[(t + T - j) % T], out_numbers[j - 1])
    total = xq[0].astype(F32)
    for k in range(1, T):
        total = total + xq[k].astype(F32)
    out[...] = total.astype(BF16)

    finish()
    for k in range(T):
        ing[:, k * chunk:(k + 1) * chunk] = igb[k]

    for copy in sent:
        copy.wait_send()

    def written(k, carry):
        at = pl.ds(pl.multiple_of(k * chunk, chunk), chunk)
        pltpu.make_async_copy(wgv.at[at, :], wg.at[at, :], local_sems.at[k]).wait()
        return carry

    lax.fori_loop(0, 8, written, 0)
    assert used[0] <= SEMS, used[0]


def per_device(activations, weight, out_grad):
    tokens, width = activations.shape
    features = weight.shape[1]
    groups = YL * Z * C
    chunk = width // T
    scale = 1.0 / math.sqrt(width * T)
    grad_scale = 1.0 / math.sqrt(tokens * groups)
    had = jnp.asarray(signs_table(chunk), BF16)
    vmem = pl.BlockSpec(memory_space=pltpu.VMEM)
    part = (T, tokens, chunk)
    return pl.pallas_call(
        functools.partial(kernel, scale, grad_scale),
        out_shape=(
            jax.ShapeDtypeStruct((out_grad.shape[0], features), BF16),
            jax.ShapeDtypeStruct((tokens, width), BF16),
            jax.ShapeDtypeStruct((width, features), F32),
        ),
        in_specs=[vmem] * 4,
        out_specs=(vmem, vmem, pl.BlockSpec(memory_space=pl.ANY)),
        scratch_shapes=[
            pltpu.VMEM((width, features), BF16),
            pltpu.VMEM(part, F32), pltpu.VMEM(part, F32), pltpu.VMEM(part, BF16),
            pltpu.VMEM((groups,) + part, BF16),
            pltpu.VMEM((groups // C, C, tokens, features), BF16),
            pltpu.VMEM((groups // C, tokens, features), BF16),
            pltpu.VMEM((groups // C,) + part, F32),
            pltpu.VMEM((2, 4) + part, BF16), pltpu.VMEM((2, 4) + part, BF16),
            pltpu.VMEM((2, 4) + part, BF16), pltpu.VMEM((2, 4) + part, BF16),
            pltpu.VMEM(part, BF16), pltpu.VMEM(part, BF16),
            pltpu.VMEM((T, out_grad.shape[0], features), BF16),
            pltpu.VMEM((T, out_grad.shape[0], features), BF16),
            pltpu.VMEM(part, F32), pltpu.VMEM(part, F32),
            pltpu.VMEM(part, BF16), pltpu.VMEM(part, BF16),
            pltpu.VMEM((width, features), F32),
            pltpu.VMEM(part, F32),
            pltpu.SemaphoreType.DMA((SEMS,)),
            pltpu.SemaphoreType.DMA((T,)),
        ],
        compiler_params=pltpu.CompilerParams(
            collective_id=0, has_side_effects=True, vmem_limit_bytes=56 << 20),
        name="rotated_projection",
    )(activations, weight, out_grad.reshape(2, C, tokens, features), had)


def solution(mesh):
    return jax.shard_map(
        per_device,
        mesh=mesh,
        in_specs=(P("dp", "tensor"), P("tensor", "dp"), P("tensor", "dp")),
        out_specs=(P("tensor", "dp"), P("dp", "tensor"), P("tensor", "dp")),
        check_vma=False,
    )
```

time: 357 us -> 105 us (0.29)
  waiting for transfers between devices: 297 us -> 0 us
  Pallas kernels: 0 us -> 96 us
  matrix products: 21.8 us -> 0 us
  starting transfers between devices: 16.9 us -> 0 us
  between operations: 13.8 us -> 0.64 us
  local copies, waits for them, and re-layouts: 2.84 us -> 7.77 us
    reduce_scatter x2 -> x0, waiting for transfers between devices: 178 us -> none  [the longest x1 121 us: per_device(): lax.psum_scatter(lax.dot_general(grad_all, weight, (((1,), (1,)), ((), ()...]
    pallas_call x0 -> x1, Pallas kernels: none -> 96 us  [per_device(): pl.pallas_call(functools.partial(kernel, scale, grad_scale), out_shape=(j...]
    all_gather x2 -> x0, waiting for transfers between devices: 93.4 us -> none  [the longest x1 62.6 us: per_device(): rows_all = lax.all_gather(rotated, 'dp', axis=0, tiled=True)]
    ppermute x6 -> x0, waiting for transfers between devices: 25.8 us -> none  [from_partner(): lax.ppermute(shard, axis, [(i, i ^ 1 << apart) for i in range(lax.axis_si...]
    dot_general x7 -> x0, matrix products: 21.8 us -> none  [the longest x1 6.9 us: per_device(): lax.dot_general(rows_all, grad_all, (((0,), (0,)), ((), ())), preferred_e...]
    ppermute x6 -> x0, starting transfers between devices: 16.7 us -> none  [from_partner(): lax.ppermute(shard, axis, [(i, i ^ 1 << apart) for i in range(lax.axis_si...]
    unnamed x2 -> x3, local copies, waits for them, and re-layouts: 0.01 us -> 7.77 us
  transfers between devices with their start and end apart: 10 -> 0, of which waited for: 9 -> 0; matrix products, arithmetic and copies ran while one was open for 7% -> 0% of each run, Pallas kernels for 0% -> 0%
where the time goes in v1:
time: 105 us; the launch traced here: 104 us
  Pallas kernels  96 us (91%)
  local copies, waits for them, and re-layouts  7.77 us (7%)
    pallas_call x1, Pallas kernels, per_device(): pl.pallas_call(functools.partial(kernel, scale, grad_scale), out_shape=(j...  96 us
    unnamed x3, local copies, waits for them, and re-layouts  7.77 us

profile of v1, /device:TPU:1, one launch (start us, length us, event | category | flops | bytes accessed | tf_op | source)
XLA Modules:
  0.0 104.4 jit_solution(12060635569471417009)
XLA Ops:
  0.6 96.0 %rotated_projection.1 = (bf16[128,512]{1,0:T(8,128)(2,1)}, bf16[32,2048]{1,0:T(8,128)(2,1)}, f32[2048,512]{1,0:T(8,128)}) custom-call(bf16[32,2048]{1,0:T(8,128)(2,1)} %act.1, bf16[2048,512]{1,0:T(8,128)(2,1)} %w.1, bf16[2,2,32,512]{3,2,1,0:T(8,128)(2,1)} %bitcast.1, bf16[256,256]{1,0:T(8,128)(2,1)} %constant.2.clone.had), custom_call_target="tpu_custom_call" | custom-call | tf_op jit(solution)/shard_map/rotated_projection/pallas_call | solution.py:289
  96.6 1.6 %copy.10 = bf16[128,512]{1,0:T(8,128)(2,1)} copy(bf16[128,512]{1,0:T(8,128)(2,1)} %get-tuple-element.6) | data formatting | bytes 262144
  98.2 1.6 %copy.11 = bf16[32,2048]{1,0:T(8,128)(2,1)} copy(bf16[32,2048]{1,0:T(8,128)(2,1)} %get-tuple-element.7) | data formatting | bytes 262144
  99.8 4.6 %copy.12 = f32[2048,512]{1,0:T(8,128)} copy(f32[2048,512]{1,0:T(8,128)} %get-tuple-element.8) | data formatting | bytes 8388608

commit v2 on v1

--- a/solution.py
+++ b/solution.py
@@ -10,9 +10,10 @@
 from jax.sharding import PartitionSpec as P
 
 MESH = pl.DeviceIdType.MESH
-YL, Z, C, T = 2, 8, 2, 8
+YL, Z, C, T, X = 2, 8, 2, 8, 4
+LO_CHUNKS = 4
 F32, BF16 = jnp.float32, jnp.bfloat16
-SEMS = 256
+SEMS = 320
 
 
 def signs_table(width):
@@ -36,26 +37,37 @@
     return parts
 
 
-def kernel(scale, grad_scale, act, w, og, had, out, ing, wg, w2, s1, x1, s2, r, g, g2, pf,
-           sbp, sbm, rp, rm, ys, yr, q, xq, t1, v1, t2, igb, wgv, rg, sems, local_sems):
+def kernel(scale, grad_scale, lo_chunks, act_hbm, w_hbm, og_hbm, had_hbm, out, ing, wg, act, w, og, had,
+           w2, s1, x1, s2, r, g, g2, pf, sbp, sbm, rp, rm, ybs, ybr, ys, yr, q, xq, t1, v1, t2, igb,
+           wgv, rg, sems, local_sems):
     d, t = lax.axis_index("dp"), lax.axis_index("tensor")
     c, z, yl = d % C, (d // C) % Z, d // (C * Z)
+    yh, x = t // X, t % X
+    ahead = 1 - 2 * c
     tokens, width = act.shape
     chunk = width // T
+    lo, hi = pl.ds(0, lo_chunks), pl.ds(lo_chunks, T - lo_chunks)
 
     def block(rel, zz, core):
         return (((yl + rel) % YL) * Z + (zz + 2 * Z) % Z) * C + core
 
     sib = (block(0, z, 1 - c), t)
-    zp, zm = (block(0, z + 1, c), t), (block(0, z - 1, c), t)
+    zp, zm = (block(0, z + ahead, c), t), (block(0, z - ahead, c), t)
     yp = (block(1, z, c), t)
     peers = [(d, (t + j) % T) for j in range(1, T)]
+    opposite = (d, (t + X) % T)
+    along_x = [(d, yh * X + (x + j) % X) for j in range(1, X)]
 
     barrier = pltpu.get_barrier_semaphore()
     everyone = [sib, zp, zm, yp] + peers
     for other in everyone:
         pl.semaphore_signal(barrier, inc=1, device_id=other, device_id_type=MESH)
-    pl.semaphore_wait(barrier, len(everyone))
+    loads = [pltpu.make_async_copy(src, dst, local_sems.at[T + i])
+             for i, (src, dst) in enumerate(((act_hbm, act), (had_hbm, had), (og_hbm, og), (w_hbm, w)))]
+    for load in loads:
+        load.start()
+    loads[0].wait()
+    loads[1].wait()
 
     used = [0]
     sent = []
@@ -92,15 +104,15 @@
                      + jnp.dot(low, table, preferred_element_type=F32))
         return butterfly([mixed[k * tokens:(k + 1) * tokens] for k in range(T)])
 
-    def rotate(parts, first, first_in, second, landing):
-        for k, part in enumerate(local_rotation(parts)):
-            first[k] = part
+    def rotate_first(first, first_in):
         numbers = [pair() for _ in peers]
         for j, peer in enumerate(peers):
             send(first.at[peer[1]], first_in.at[t], peer, numbers[j])
         first_in[t] = first[t]
         for j in range(1, T):
             arrive(first_in.at[(t + T - j) % T], numbers[j - 1])
+
+    def rotate_second(first_in, second, landing):
         for k, part in enumerate(butterfly([first_in[k] for k in range(T)])):
             second[k] = (part * scale).astype(BF16)
         numbers = [pair() for _ in peers]
@@ -114,41 +126,68 @@
 
         return finish
 
+    own = block(0, z, c)
+    for k, part in enumerate(local_rotation([act[:, k * chunk:(k + 1) * chunk] for k in range(T)])):
+        s1[k] = part
+    pl.semaphore_wait(barrier, len(everyone))
+    rotate_first(s1, x1)
+    loads[2].wait()
+
+    def grad_rows(tt):
+        return g.at[pl.ds(2 * tt, 2)]
+
+    opposite_number = pair()
+    send(og, grad_rows(t), opposite, opposite_number)
+    finish = rotate_second(x1, s2, r.at[own])
+    near_numbers = [pair() for _ in along_x]
+    for j, peer in enumerate(along_x):
+        send(og, grad_rows(t), peer, near_numbers[j])
+    g[pl.ds(2 * t, 2)] = og[...]
+    loads[3].wait()
     w_number = pair()
     send(w, w2, sib, w_number)
-
-    own = block(0, z, c)
-    finish = rotate([act[:, k * chunk:(k + 1) * chunk] for k in range(T)], s1, x1, s2, r.at[own])
-
-    gather_numbers = [pair() for _ in peers]
-    for j, peer in enumerate(peers):
-        send(og, g.at[pl.ds(2 * t, 2)], peer, gather_numbers[j])
-    g[pl.ds(2 * t, 2)] = og[...]
-
     finish()
 
     to_sib = []
 
-    def share(rel, zz):
+    def share(rel, zz, part):
         number = pair()
-        send(r.at[block(rel, zz, c)], r.at[block(rel, zz, c)], sib, number)
-        to_sib.append((block(rel, zz, 1 - c), number))
+        send(r.at[block(rel, zz, c), part], r.at[block(rel, zz, c), part], sib, number)
+        to_sib.append((block(rel, zz, 1 - c), part, number))
 
     numbers = {(sign, rel, s): pair() for sign in (1, -1) for rel in (0, 1) for s in range(4)}
+    whole = pl.ds(0, T)
+    parts = (whole, lo)
+    across_numbers = {}
 
     def pass_on(sign, rel, zz, s):
-        b = block(rel, zz, c)
-        send(r.at[b], r.at[b], zp if sign == 1 else zm, numbers[sign, rel, s])
+        view = r.at[block(rel, zz, c), parts[rel]]
+        send(view, view, zp if sign == 1 else zm, numbers[sign, rel, s])
+
+    def across(zz, step):
+        across_numbers[step] = pair()
+        view = r.at[block(0, zz, c), hi]
+        send(view, view, yp, across_numbers[step])
+
+    def across_arrive(zz, step):
+        arrive(r.at[block(1, zz, c), hi], across_numbers[step])
+        share(1, zz, hi)
 
     y_number = pair()
-    send(r.at[own], r.at[own], yp, y_number)
+    send(r.at[own, lo], r.at[own, lo], yp, y_number)
     pass_on(1, 0, z, 0)
     pass_on(-1, 0, z, 0)
-    share(0, z)
-    arrive(r.at[block(1, z, c)], y_number)
+    across(z, 0)
+    share(0, z, whole)
+    opposite_t = (t + X) % T
+    arrive(grad_rows(opposite_t), opposite_number)
+    far_numbers = [pair() for _ in along_x]
+    for j, peer in enumerate(along_x):
+        send(grad_rows(opposite_t), grad_rows(opposite_t), peer, far_numbers[j])
+    arrive(r.at[block(1, z, c), lo], y_number)
     pass_on(1, 1, z, 0)
     pass_on(-1, 1, z, 0)
-    share(1, z)
+    share(1, z, lo)
 
     def ring_step(s):
         for rel in (0, 1):
@@ -156,17 +195,27 @@
                 keep = 0 if sign == 1 else 1
                 if s == 3 and rel != keep:
                     continue
-                zz = z - sign * (1 + s)
-                arrive(r.at[block(rel, zz, c)], numbers[sign, rel, s])
+                zz = z - sign * ahead * (1 + s)
+                arrive(r.at[block(rel, zz, c), parts[rel]], numbers[sign, rel, s])
                 if s < 2 or (s == 2 and rel == keep):
                     pass_on(sign, rel, zz, s + 1)
-                share(rel, zz)
+                if rel == 0:
+                    across(zz, sign * (1 + s))
+                share(rel, zz, parts[rel])
+
+    def across_step(s):
+        for sign in (1, -1):
+            if s < 3 or sign == 1:
+                across_arrive(z - sign * ahead * (1 + s), sign * (1 + s))
 
     ring_step(0)
-    for j in range(1, T):
-        arrive(g.at[pl.ds(2 * ((t + T - j) % T), 2)], gather_numbers[j - 1])
+    for j in range(1, X):
+        from_x = (x + X - j) % X
+        arrive(grad_rows(yh * X + from_x), near_numbers[j - 1])
+        arrive(grad_rows((1 - yh) * X + from_x), far_numbers[j - 1])
     g2_number = pair()
     send(g.at[:, 1 - c], g2, sib, g2_number)
+    across_arrive(z, 0)
     ring_step(1)
     arrive(g2, g2_number)
     arrive(w2, w_number)
@@ -184,9 +233,18 @@
         return carry
 
     lax.fori_loop(0, T, partial, 0)
-    ring_step(2)
 
     sums = {(sign, rel, s): pair() for sign in (1, -1) for rel in (0, 1) for s in range(4)}
+    back_numbers = {}
+
+    def target(rel, zz):
+        return block(rel, zz, 0) // C
+
+    def give_across(away):
+        i = away + 4
+        ybs[i] = pf[target(1, z + ahead * away), hi].astype(BF16)
+        back_numbers[away] = pair()
+        send(ybs.at[i], ybr.at[i], yp, back_numbers[away])
 
     def reduce_step(s):
         for rel in (0, 1):
@@ -195,18 +253,32 @@
                 if s == 0 and rel != keep:
                     continue
                 into, out_of, to = (rp, sbp, zp) if sign == 1 else (rm, sbm, zm)
-                target = block(rel, z + sign * (4 - s), 0) // C
-                total = pf[target]
-                if s > 1 or (s == 1 and rel == keep):
-                    arrive(into.at[rel, s - 1], sums[sign, rel, s - 1])
-                    total = total + into[rel, s - 1].astype(F32)
-                out_of[rel, s] = total.astype(BF16)
-                send(out_of.at[rel, s], into.at[rel, s], to, sums[sign, rel, s])
-
+                away = sign * (4 - s)
+                at = target(rel, z + ahead * away)
+                more = s > 1 or (s == 1 and rel == keep)
+                if more:
+                    arrive(into.at[rel, s - 1, parts[rel]], sums[sign, rel, s - 1])
+                total = pf[at, lo]
+                if more:
+                    total = total + into[rel, s - 1, lo].astype(F32)
+                out_of[rel, s, lo] = total.astype(BF16)
+                if rel == 0:
+                    arrive(ybr.at[away + 4], back_numbers[away])
+                    total = pf[at, hi] + ybr[away + 4].astype(F32)
+                    if more:
+                        total = total + into[rel, s - 1, hi].astype(F32)
+                    out_of[rel, s, hi] = total.astype(BF16)
+                send(out_of.at[rel, s, parts[rel]], into.at[rel, s, parts[rel]], to, sums[sign, rel, s])
+
+    for away in (4, 3, -3, 2, -2, 1, -1, 0):
+        give_across(away)
     reduce_step(0)
+    ring_step(2)
+    across_step(0)
+    reduce_step(1)
     ring_step(3)
-    for b, number in to_sib:
-        arrive(r.at[b], number)
+    across_step(1)
+    across_step(2)
 
     def products(i, carry):
         total = jnp.zeros((256, w.shape[1]), F32)
@@ -215,12 +287,6 @@
             total = total + jnp.dot(lhs, w[k * chunk:(k + 1) * chunk, :], preferred_element_type=F32)
         q[pl.ds(2 * i, 2)] = total.reshape(2, 128, w.shape[1]).astype(BF16)
         return carry
-
-    lax.fori_loop(0, 4, products, 0)
-    out_numbers = [pair() for _ in peers]
-    for j, peer in enumerate(peers):
-        send(q.at[peer[1]], xq.at[t], peer, out_numbers[j])
-    xq[t] = q[t]
 
     def weight_grad(k, carry):
         lhs = r[:, k].reshape(2 * rows, chunk)
@@ -231,27 +297,40 @@
         pltpu.make_async_copy(wgv.at[at, :], wg.at[at, :], local_sems.at[k]).start()
         return carry
 
-    reduce_step(1)
-    lax.fori_loop(0, 3, weight_grad, 0)
+    across_step(3)
+    for b, part, number in to_sib:
+        arrive(r.at[b, part], number)
+    lax.fori_loop(0, 4, products, 0)
+    out_numbers = [pair() for _ in peers]
+    for j, peer in enumerate(peers):
+        send(q.at[peer[1]], xq.at[t], peer, out_numbers[j])
+    xq[t] = q[t]
+
     reduce_step(2)
-    lax.fori_loop(3, 6, weight_grad, 0)
+    lax.fori_loop(0, 4, weight_grad, 0)
     reduce_step(3)
-    lax.fori_loop(6, 8, weight_grad, 0)
-
-    finals = []
-    for rel in (1, 0):
-        total = pf[block(rel, z, 0) // C]
-        for sign, into in ((1, rp), (-1, rm)):
-            arrive(into.at[rel, 3], sums[sign, rel, 3])
-            total = total + into[rel, 3].astype(F32)
-        if rel == 1:
-            ys[...] = total.astype(BF16)
-            back_number = pair()
-            send(ys, yr, yp, back_number)
-        else:
-            rg[...] = total
+    lax.fori_loop(4, 8, weight_grad, 0)
+
+    total = pf[target(1, z), lo]
+    for sign, into in ((1, rp), (-1, rm)):
+        arrive(into.at[1, 3, lo], sums[sign, 1, 3])
+        total = total + into[1, 3, lo].astype(F32)
+    ys[...] = total.astype(BF16)
+    back_number = pair()
+    send(ys, yr, yp, back_number)
+    total = pf[target(0, z)]
+    for sign, into in ((1, rp), (-1, rm)):
+        arrive(into.at[0, 3], sums[sign, 0, 3])
+        total = total + into[0, 3].astype(F32)
+    rg[...] = total
+    arrive(ybr.at[4], back_numbers[0])
+    rg[hi] = rg[hi] + ybr[4].astype(F32)
     arrive(yr, back_number)
-    finish = rotate([rg[k] + yr[k].astype(F32) for k in range(T)], t1, v1, t2, igb)
+    rg[lo] = rg[lo] + yr[...].astype(F32)
+    for k, part in enumerate(local_rotation([rg[k] for k in range(T)])):
+        t1[k] = part
+    rotate_first(t1, v1)
+    finish = rotate_second(v1, t2, igb)
 
     for j in range(1, T):
         arrive(xq.at[(t + T - j) % T], out_numbers[j - 1])
@@ -274,6 +353,21 @@
 
     lax.fori_loop(0, 8, written, 0)
     assert used[0] <= SEMS, used[0]
+
+
+def place(pieces, *refs):
+    sems = refs[-1]
+    half = (len(refs) - 1) // 2
+    copies = []
+    for src, dst, count in zip(refs[:half], refs[half:2 * half], pieces):
+        step = src.shape[0] // count
+        for i in range(count):
+            at = pl.ds(i * step, step)
+            copies.append(pltpu.make_async_copy(src.at[at], dst.at[at], sems.at[len(copies)]))
+    for copy in copies:
+        copy.start()
+    for copy in copies:
+        copy.wait()
 
 
 def per_device(activations, weight, out_grad):
@@ -285,17 +379,25 @@
     grad_scale = 1.0 / math.sqrt(tokens * groups)
     had = jnp.asarray(signs_table(chunk), BF16)
     vmem = pl.BlockSpec(memory_space=pltpu.VMEM)
+    anywhere = pl.BlockSpec(memory_space=pl.ANY)
     part = (T, tokens, chunk)
-    return pl.pallas_call(
-        functools.partial(kernel, scale, grad_scale),
-        out_shape=(
-            jax.ShapeDtypeStruct((out_grad.shape[0], features), BF16),
-            jax.ShapeDtypeStruct((tokens, width), BF16),
-            jax.ShapeDtypeStruct((width, features), F32),
-        ),
-        in_specs=[vmem] * 4,
-        out_specs=(vmem, vmem, pl.BlockSpec(memory_space=pl.ANY)),
+    low = (LO_CHUNKS, tokens, chunk)
+    high = (T - LO_CHUNKS, tokens, chunk)
+    shapes = (
+        jax.ShapeDtypeStruct((out_grad.shape[0], features), BF16),
+        jax.ShapeDtypeStruct((tokens, width), BF16),
+        jax.ShapeDtypeStruct((width, features), F32),
+    )
+    results = pl.pallas_call(
+        functools.partial(kernel, scale, grad_scale, LO_CHUNKS),
+        out_shape=shapes,
+        in_specs=[anywhere] * 4,
+        out_specs=(vmem, vmem, anywhere),
         scratch_shapes=[
+            pltpu.VMEM((tokens, width), BF16),
+            pltpu.VMEM((width, features), BF16),
+            pltpu.VMEM((2, C, tokens, features), BF16),
+            pltpu.VMEM((chunk, chunk), BF16),
             pltpu.VMEM((width, features), BF16),
             pltpu.VMEM(part, F32), pltpu.VMEM(part, F32), pltpu.VMEM(part, BF16),
             pltpu.VMEM((groups,) + part, BF16),
@@ -304,7 +406,8 @@
             pltpu.VMEM((groups // C,) + part, F32),
             pltpu.VMEM((2, 4) + part, BF16), pltpu.VMEM((2, 4) + part, BF16),
             pltpu.VMEM((2, 4) + part, BF16), pltpu.VMEM((2, 4) + part, BF16),
-            pltpu.VMEM(part, BF16), pltpu.VMEM(part, BF16),
+            pltpu.VMEM((9,) + high, BF16), pltpu.VMEM((9,) + high, BF16),
+            pltpu.VMEM(low, BF16), pltpu.VMEM(low, BF16),
             pltpu.VMEM((T, out_grad.shape[0], features), BF16),
             pltpu.VMEM((T, out_grad.shape[0], features), BF16),
             pltpu.VMEM(part, F32), pltpu.VMEM(part, F32),
@@ -312,12 +415,21 @@
             pltpu.VMEM((width, features), F32),
             pltpu.VMEM(part, F32),
             pltpu.SemaphoreType.DMA((SEMS,)),
-            pltpu.SemaphoreType.DMA((T,)),
+            pltpu.SemaphoreType.DMA((T + 4,)),
         ],
         compiler_params=pltpu.CompilerParams(
             collective_id=0, has_side_effects=True, vmem_limit_bytes=56 << 20),
         name="rotated_projection",
     )(activations, weight, out_grad.reshape(2, C, tokens, features), had)
+    pieces = (1, 1, 8)
+    return pl.pallas_call(
+        functools.partial(place, pieces),
+        out_shape=shapes,
+        in_specs=[anywhere] * 3,
+        out_specs=(anywhere,) * 3,
+        scratch_shapes=[pltpu.SemaphoreType.DMA((sum(pieces),))],
+        name="place_results",
+    )(*results)
 
 
 def solution(mesh):

time: 105 us -> 225 us (2.14)
  Pallas kernels: 96 us -> 224 us
  local copies, waits for them, and re-layouts: 7.77 us -> 0 us
    pallas_call x1 -> x2, Pallas kernels: 96 us -> 224 us  [the longest x1 136 us: per_device(): pl.pallas_call(functools.partial(place, pieces), out_shape=shapes, in_spe...]
    unnamed x3 -> x0, local copies, waits for them, and re-layouts: 7.77 us -> none
where the time goes in v2:
time: 225 us
  Pallas kernels  224 us (100%)
    pallas_call x1, Pallas kernels, per_device(): pl.pallas_call(functools.partial(place, pieces), out_shape=shapes, in_spe...  136 us
    pallas_call x1, Pallas kernels, per_device(): pl.pallas_call(functools.partial(kernel, scale, grad_scale, LO_CHUNKS), o...  87.7 us

profile of v2, /device:TPU:1, one launch (start us, length us, event | category | flops | bytes accessed | tf_op | source)
XLA Modules:
  0.0 224.5 jit_solution(2113123375334840004)
XLA Ops:
  0.6 87.7 %rotated_projection.1 = (bf16[128,512]{1,0:T(8,128)(2,1)}, bf16[32,2048]{1,0:T(8,128)(2,1)}, f32[2048,512]{1,0:T(8,128)}) custom-call(bf16[32,2048]{1,0:T(8,128)(2,1)} %act_hbm.1, bf16[2048,512]{1,0:T(8,128)(2,1)} %w_hbm.1, bf16[2,2,32,512]{3,2,1,0:T(8,128)(2,1)} %bitcast.1, bf16[256,256]{1,0:T(8,128)(2,1)} %constant.2.clone.had_hbm), custom_call_target="tpu_custom_call" | custom-call | tf_op jit(solution)/shard_map/rotated_projection/pallas_call | solution.py:391
  88.3 136.2 %place_results.1 = (bf16[128,512]{1,0:T(8,128)(2,1)}, bf16[32,2048]{1,0:T(8,128)(2,1)}, f32[2048,512]{1,0:T(8,128)}) custom-call(bf16[128,512]{1,0:T(8,128)(2,1)} %get-tuple-element.6.refs_0_, bf16[32,2048]{1,0:T(8,128)(2,1)} %get-tuple-element.7.refs_1_, f32[2048,512]{1,0:T(8,128)} %get-tuple-element.8.refs_2_), custom_call_target="tpu_custom_call" | custom-call | tf_op jit(solution)/shard_map/place_results/pallas_call | solution.py:425

commit v3 on v2

v3 whole, which is shorter than its diff:
```python
import functools
import math

import jax
import jax.numpy as jnp
import numpy as np
from jax import lax
from jax.experimental import pallas as pl
from jax.experimental.pallas import tpu as pltpu
from jax.sharding import PartitionSpec as P

MESH = pl.DeviceIdType.MESH
YL, Z, C, T, X = 2, 8, 2, 8, 4
LO_CHUNKS = 4
F32, BF16 = jnp.float32, jnp.bfloat16
SEMS = 320


def signs_table(width):
    position = np.arange(width)
    joined = position[:, None] & position[None, :]
    parity = np.zeros_like(joined)
    for bit_number in range(width.bit_length() - 1):
        parity = parity + ((joined >> bit_number) & 1)
    return np.where(parity % 2 == 1, -1.0, 1.0)


def butterfly(parts):
    parts = list(parts)
    apart = 1
    while apart < len(parts):
        for low in range(len(parts)):
            if low & apart == 0:
                a, b = parts[low], parts[low | apart]
                parts[low], parts[low | apart] = a + b, a - b
        apart *= 2
    return parts


def kernel(scale, grad_scale, lo_chunks, act_hbm, w_hbm, og_hbm, had_hbm, out, ing, wg, act, w, og, had,
           w2, s1, x1, s2, r, g, g2, pf, sbp, sbm, rp, rm, ybs, ybr, ys, yr, q, xq, os, oa, t1, v1, t2, igb,
           rg, sems, local_sems):
    d, t = lax.axis_index("dp"), lax.axis_index("tensor")
    c, z, yl = d % C, (d // C) % Z, d // (C * Z)
    yh, x = t // X, t % X
    ahead = 1 - 2 * c
    tokens, width = act.shape
    chunk = width // T
    lo, hi = pl.ds(0, lo_chunks), pl.ds(lo_chunks, T - lo_chunks)

    def block(rel, zz, core):
        return (((yl + rel) % YL) * Z + (zz + 2 * Z) % Z) * C + core

    sib = (block(0, z, 1 - c), t)
    zp, zm = (block(0, z + ahead, c), t), (block(0, z - ahead, c), t)
    yp = (block(1, z, c), t)
    peers = [(d, (t + j) % T) for j in range(1, T)]
    opposite = (d, (t + X) % T)
    along_x = [(d, yh * X + (x + j) % X) for j in range(1, X)]

    barrier = pltpu.get_barrier_semaphore()
    everyone = [sib, zp, zm, yp] + peers
    for other in everyone:
        pl.semaphore_signal(barrier, inc=1, device_id=other, device_id_type=MESH)
    loads = [pltpu.make_async_copy(src, dst, local_sems.at[T + i])
             for i, (src, dst) in enumerate(((act_hbm, act), (had_hbm, had), (og_hbm, og), (w_hbm, w)))]
    for load in loads:
        load.start()
    loads[0].wait()
    loads[1].wait()

    used = [0]
    sent = []

    def pair():
        used[0] += 2
        return used[0] - 2

    def remote(src, dst, to, number):
        return pltpu.make_async_remote_copy(
            src_ref=src, dst_ref=dst, send_sem=sems.at[number], recv_sem=sems.at[number + 1],
            device_id=to, device_id_type=MESH)

    def send(src, dst, to, number):
        copy = remote(src, dst, to, number)
        copy.start()
        sent.append(copy)

    def arrive(dst, number):
        remote(dst, dst, sib, number).wait_recv()

    def local_rotation(parts):
        rows = jnp.concatenate(parts, axis=0)
        table = had[...]
        if rows.dtype == BF16:
            mixed = jnp.dot(rows, table, preferred_element_type=F32)
        else:
            high = rows.astype(BF16)
            rest = rows - high.astype(F32)
            middle = rest.astype(BF16)
            low = (rest - middle.astype(F32)).astype(BF16)
            mixed = (jnp.dot(high, table, preferred_element_type=F32)
                     + jnp.dot(middle, table, preferred_element_type=F32)
                     + jnp.dot(low, table, preferred_element_type=F32))
        return butterfly([mixed[k * tokens:(k + 1) * tokens] for k in range(T)])

    def rotate_first(first, first_in):
        numbers = [pair() for _ in peers]
        for j, peer in enumerate(peers):
            send(first.at[peer[1]], first_in.at[t], peer, numbers[j])
        first_in[t] = first[t]

        def finish():
            for j in range(1, T):
                arrive(first_in.at[(t + T - j) % T], numbers[j - 1])

        return finish

    def rotate_second(first_in, second, landing):
        for k, part in enumerate(butterfly([first_in[k].astype(F32) for k in range(T)])):
            second[k] = (part * scale).astype(BF16)
        numbers = [pair() for _ in peers]
        for j, peer in enumerate(peers):
            send(second.at[peer[1]], landing.at[t], peer, numbers[j])
        landing[t] = second[t]

        def finish():
            for j in range(1, T):
                arrive(landing.at[(t + T - j) % T], numbers[j - 1])

        return finish

    own = block(0, z, c)
    for k, part in enumerate(local_rotation([act[:, k * chunk:(k + 1) * chunk] for k in range(T)])):
        s1[k] = part
    pl.semaphore_wait(barrier, len(everyone))
    first_done = rotate_first(s1, x1)
    loads[2].wait()

    def grad_rows(tt):
        return g.at[pl.ds(2 * tt, 2)]

    opposite_number = pair()
    send(og, grad_rows(t), opposite, opposite_number)
    g[pl.ds(2 * t, 2)] = og[...]
    loads[3].wait()
    w_number = pair()
    send(w, w2, sib, w_number)
    first_done()
    finish = rotate_second(x1, s2, r.at[own])
    near_numbers = [pair() for _ in along_x]
    for j, peer in enumerate(along_x):
        send(og, grad_rows(t), peer, near_numbers[j])
    opposite_t = (t + X) % T
    arrive(grad_rows(opposite_t), opposite_number)
    far_numbers = [pair() for _ in along_x]
    for j, peer in enumerate(along_x):
        send(grad_rows(opposite_t), grad_rows(opposite_t), peer, far_numbers[j])
    finish()

    to_sib = []

    def share(rel, zz, part):
        number = pair()
        send(r.at[block(rel, zz, c), part], r.at[block(rel, zz, c), part], sib, number)
        to_sib.append((block(rel, zz, 1 - c), part, number))

    pieces = ((0, "hi", 1), (1, "lo", 1), (0, "lo", -1))
    halves = {"lo": lo, "hi": hi}
    numbers = {(sign, piece, s): pair() for sign in (1, -1) for piece in pieces for s in range(4)}
    across_numbers = {}

    def pass_on(sign, piece, zz, s):
        view = r.at[block(piece[0], zz, c), halves[piece[1]]]
        send(view, view, zp if sign == 1 else zm, numbers[sign, piece, s])

    def across(zz, step):
        across_numbers[step] = pair()
        view = r.at[block(0, zz, c), hi]
        send(view, view, yp, across_numbers[step])

    def across_arrive(zz, step):
        arrive(r.at[block(1, zz, c), hi], across_numbers[step])
        share(1, zz, hi)

    y_number = pair()
    send(r.at[own, lo], r.at[own, lo], yp, y_number)
    for piece in pieces:
        if piece[0] == 0:
            pass_on(1, piece, z, 0)
            pass_on(-1, piece, z, 0)
    share(0, z, lo)
    share(0, z, hi)
    arrive(r.at[block(1, z, c), lo], y_number)
    pass_on(1, pieces[1], z, 0)
    pass_on(-1, pieces[1], z, 0)
    share(1, z, lo)

    def ring_piece(s, piece):
        rel, half, far = piece
        for sign in (1, -1):
            if s == 3 and sign != far:
                continue
            zz = z - sign * ahead * (1 + s)
            arrive(r.at[block(rel, zz, c), halves[half]], numbers[sign, piece, s])
            if s < 2 or (s == 2 and sign == far):
                pass_on(sign, piece, zz, s + 1)
            share(rel, zz, halves[half])

    def ring_step(s):
        for piece in pieces:
            ring_piece(s, piece)

    def across_send(s):
        for sign in (1, -1):
            if s < 3 or sign == 1:
                across(z - sign * ahead * (1 + s), sign * (1 + s))

    def across_step(s):
        for sign in (1, -1):
            if s < 3 or sign == 1:
                across_arrive(z - sign * ahead * (1 + s), sign * (1 + s))

    ring_piece(0, pieces[0])
    ring_piece(0, pieces[2])
    for j in range(1, X):
        from_x = (x + X - j) % X
        arrive(grad_rows(yh * X + from_x), near_numbers[j - 1])
        arrive(grad_rows((1 - yh) * X + from_x), far_numbers[j - 1])
    g2_number = pair()
    send(g.at[:, 1 - c], g2, sib, g2_number)
    ring_piece(0, pieces[1])
    arrive(g2, g2_number)
    arrive(w2, w_number)

    rows = Z * YL * tokens

    def partial(k, carry):
        mine = g[:, c].reshape(rows, g.shape[-1])
        theirs = g2[...].reshape(rows, g.shape[-1])
        at = pl.ds(pl.multiple_of(k * chunk, chunk), chunk)
        dims = (((1,), (1,)), ((), ()))
        total = (lax.dot_general(mine, w[at, :], dims, preferred_element_type=F32)
                 + lax.dot_general(theirs, w2[at, :], dims, preferred_element_type=F32))
        pf[:, k] = total.reshape(Z * YL, tokens, chunk)
        return carry

    sums = {(sign, piece, s): pair() for sign in (1, -1) for piece in pieces for s in range(4)}
    back_numbers = {}

    def target(rel, zz):
        return block(rel, zz, 0) // C

    def give_across(away):
        i = away + 4
        ybs[i] = pf[target(1, z + ahead * away), hi].astype(BF16)
        back_numbers[away] = pair()
        send(ybs.at[i], ybr.at[i], yp, back_numbers[away])

    def reduce_piece(s, piece):
        rel, half, far = piece
        part = halves[half]
        for sign in (1, -1):
            if s == 0 and sign != far:
                continue
            into, out_of, to = (rp, sbp, zp) if sign == 1 else (rm, sbm, zm)
            away = sign * (4 - s)
            total = pf[target(rel, z + ahead * away), part]
            if half == "hi":
                arrive(ybr.at[away + 4], back_numbers[away])
                total = total + ybr[away + 4].astype(F32)
            if s > 1 or (s == 1 and sign == far):
                arrive(into.at[rel, s - 1, part], sums[sign, piece, s - 1])
                total = total + into[rel, s - 1, part].astype(F32)
            out_of[rel, s, part] = total.astype(BF16)
            send(out_of.at[rel, s, part], into.at[rel, s, part], to, sums[sign, piece, s])

    order = (pieces[1], pieces[2], pieces[0])

    def reduce_step(s):
        for piece in order:
            reduce_piece(s, piece)

    lax.fori_loop(lo_chunks, T, partial, 0)
    for away in (4, 3, -3, 2, -2, 1, -1, 0):
        give_across(away)
    lax.fori_loop(0, lo_chunks, partial, 0)
    reduce_piece(0, order[0])
    reduce_piece(0, order[1])
    ring_step(1)
    reduce_piece(0, order[2])
    across(z, 0)
    across_send(0)
    reduce_step(1)
    ring_step(2)
    across_send(1)
    across_send(2)
    reduce_step(2)
    ring_step(3)
    across_send(3)
    across_arrive(z, 0)
    across_step(0)
    reduce_step(3)
    across_step(1)
    across_step(2)

    def products(i, carry):
        total = jnp.zeros((256, w.shape[1]), F32)
        for k in range(T):
            lhs = r[pl.ds(8 * i, 8), k].reshape(256, chunk)
            total = total + jnp.dot(lhs, w[k * chunk:(k + 1) * chunk, :], preferred_element_type=F32)
        q[i // 2, pl.ds(2 * (i % 2), 2)] = total.reshape(2, 128, w.shape[1]).astype(BF16)
        return carry

    def weight_grad(k, carry):
        lhs = r[:, k].reshape(2 * rows, chunk)
        rhs = g[...].reshape(2 * rows, g.shape[-1])
        total = lax.dot_general(lhs, rhs, (((0,), (0,)), ((), ())), preferred_element_type=F32)
        at = pl.ds(pl.multiple_of(k * chunk, chunk), chunk)
        wg[at, :] = total * grad_scale
        return carry

    across_step(3)
    for b, part, number in to_sib:
        arrive(r.at[b, part], number)
    lax.fori_loop(0, 4, products, 0)
    out_numbers = [pair() for _ in along_x]
    for j, peer in enumerate(along_x):
        send(q.at[:, (x + j + 1) % X], xq.at[x], peer, out_numbers[j])
    xq[x] = q[:, x]
    lax.fori_loop(0, 3, weight_grad, 0)

    def finals(piece):
        rel, half, far = piece
        part = halves[half]
        total = pf[target(rel, z), part]
        for sign, into in ((1, rp), (-1, rm)):
            arrive(into.at[rel, 3, part], sums[sign, piece, 3])
            total = total + into[rel, 3, part].astype(F32)
        return total

    ys[...] = finals(order[0]).astype(BF16)
    back_number = pair()
    send(ys, yr, yp, back_number)
    rg[lo] = finals(order[1])
    arrive(ybr.at[4], back_numbers[0])
    rg[hi] = finals(order[2]) + ybr[4].astype(F32)
    lax.fori_loop(3, 5, weight_grad, 0)
    arrive(yr, back_number)
    rg[lo] = rg[lo] + yr[...].astype(F32)
    for k, part in enumerate(local_rotation([rg[k] for k in range(T)])):
        t1[k] = part.astype(BF16)
    first_done = rotate_first(t1, v1)
    lax.fori_loop(5, 8, weight_grad, 0)
    first_done()
    finish = rotate_second(v1, t2, igb)

    def out_sum(half):
        total = xq[0, half].astype(F32)
        for k in range(1, X):
            total = total + xq[k, half].astype(F32)
        return total

    for j in range(1, X):
        arrive(xq.at[(x + X - j) % X], out_numbers[j - 1])
    os[...] = out_sum(1 - yh).astype(BF16)
    last_number = pair()
    send(os, oa, opposite, last_number)
    total = out_sum(yh)
    arrive(oa, last_number)
    out[...] = (total + oa[...].astype(F32)).astype(BF16)

    finish()
    for k in range(T):
        ing[:, k * chunk:(k + 1) * chunk] = igb[k]

    for copy in sent:
        copy.wait_send()

    assert used[0] <= SEMS, used[0]


def place(out_in, ing_in, wg_in, out, ing, wg, sems):
    rows = wg.shape[0] // T
    copies = [pltpu.make_async_copy(out_in, out, sems.at[T]),
              pltpu.make_async_copy(ing_in, ing, sems.at[T + 1])]
    for i in range(T):
        at = pl.ds(i * rows, rows)
        copies.append(pltpu.make_async_copy(wg_in.at[at], wg.at[at], sems.at[i]))
    for copy in copies:
        copy.start()
    for copy in copies:
        copy.wait()


def per_device(activations, weight, out_grad):
    tokens, width = activations.shape
    features = weight.shape[1]
    groups = YL * Z * C
    chunk = width // T
    scale = 1.0 / math.sqrt(width * T)
    grad_scale = 1.0 / math.sqrt(tokens * groups)
    had = jnp.asarray(signs_table(chunk), BF16)
    vmem = pl.BlockSpec(memory_space=pltpu.VMEM)
    anywhere = pl.BlockSpec(memory_space=pl.ANY)
    part = (T, tokens, chunk)
    low = (LO_CHUNKS, tokens, chunk)
    high = (T - LO_CHUNKS, tokens, chunk)
    shapes = (
        jax.ShapeDtypeStruct((out_grad.shape[0], features), BF16),
        jax.ShapeDtypeStruct((tokens, width), BF16),
        jax.ShapeDtypeStruct((width, features), F32),
    )
    results = pl.pallas_call(
        functools.partial(kernel, scale, grad_scale, LO_CHUNKS),
        out_shape=tuple(pltpu.VMEM(leaf.shape, leaf.dtype) for leaf in shapes),
        in_specs=[pl.BlockSpec(memory_space=pltpu.HBM)] * 4,
        out_specs=(vmem,) * 3,
        scratch_shapes=[
            pltpu.VMEM((tokens, width), BF16),
            pltpu.VMEM((width, features), BF16),
            pltpu.VMEM((2, C, tokens, features), BF16),
            pltpu.VMEM((chunk, chunk), BF16),
            pltpu.VMEM((width, features), BF16),
            pltpu.VMEM(part, F32), pltpu.VMEM(part, F32), pltpu.VMEM(part, BF16),
            pltpu.VMEM((groups,) + part, BF16),
            pltpu.VMEM((groups // C, C, tokens, features), BF16),
            pltpu.VMEM((groups // C, tokens, features), BF16),
            pltpu.VMEM((groups // C,) + part, F32),
            pltpu.VMEM((2, 4) + part, BF16), pltpu.VMEM((2, 4) + part, BF16),
            pltpu.VMEM((2, 4) + part, BF16), pltpu.VMEM((2, 4) + part, BF16),
            pltpu.VMEM((9,) + high, BF16), pltpu.VMEM((9,) + high, BF16),
            pltpu.VMEM(low, BF16), pltpu.VMEM(low, BF16),
            pltpu.VMEM((T // X, X, out_grad.shape[0], features), BF16),
            pltpu.VMEM((X, T // X, out_grad.shape[0], features), BF16),
            pltpu.VMEM((out_grad.shape[0], features), BF16),
            pltpu.VMEM((out_grad.shape[0], features), BF16),
            pltpu.VMEM(part, BF16), pltpu.VMEM(part, BF16),
            pltpu.VMEM(part, BF16), pltpu.VMEM(part, BF16),
                pltpu.VMEM(part, F32),
            pltpu.SemaphoreType.DMA((SEMS,)),
            pltpu.SemaphoreType.DMA((T + 4,)),
        ],
        compiler_params=pltpu.CompilerParams(
            collective_id=0, has_side_effects=True, vmem_limit_bytes=237 << 18),
        name="rotated_projection",
    )(activations, weight, out_grad.reshape(2, C, tokens, features), had)
    return pl.pallas_call(
        place,
        out_shape=shapes,
        in_specs=[vmem] * 3,
        out_specs=(anywhere,) * 3,
        scratch_shapes=[pltpu.SemaphoreType.DMA((T + 2,))],
        compiler_params=pltpu.CompilerParams(vmem_limit_bytes=16 << 20),
        name="place_results",
    )(*results)


def solution(mesh):
    return jax.shard_map(
        per_device,
        mesh=mesh,
        in_specs=(P("dp", "tensor"), P("tensor", "dp"), P("tensor", "dp")),
        out_specs=(P("tensor", "dp"), P("dp", "tensor"), P("tensor", "dp")),
        check_vma=False,
    )
```

time: 225 us -> 88 us (0.39)
  Pallas kernels: 224 us -> 86.9 us
    pallas_call x1, Pallas kernels: 136 us -> 2.18 us  [per_device(): pl.pallas_call(place, out_shape=shapes, in_specs=[vmem] * 3, out_specs=(a...]
    pallas_call x1, Pallas kernels: 87.7 us -> 84.7 us  [per_device(): pl.pallas_call(functools.partial(kernel, scale, grad_scale, LO_CHUNKS), o...]
where the time goes in v3:
time: 88 us; the launch traced here: 87.5 us
  Pallas kernels  86.9 us (99%)
    pallas_call x1, Pallas kernels, per_device(): pl.pallas_call(functools.partial(kernel, scale, grad_scale, LO_CHUNKS), o...  84.7 us
    pallas_call x1, Pallas kernels, per_device(): pl.pallas_call(place, out_shape=shapes, in_specs=[vmem] * 3, out_specs=(a...  2.18 us

profile of v3, /device:TPU:1, one launch (start us, length us, event | category | flops | bytes accessed | tf_op | source)
XLA Modules:
  0.0 87.5 jit_solution(3115547240568306022)
XLA Ops:
  0.6 84.7 %rotated_projection.1 = (bf16[128,512]{1,0:T(8,128)(2,1)S(1)}, bf16[32,2048]{1,0:T(8,128)(2,1)S(1)}, f32[2048,512]{1,0:T(8,128)S(1)}) custom-call(bf16[32,2048]{1,0:T(8,128)(2,1)} %act_hbm.1, bf16[2048,512]{1,0:T(8,128)(2,1)} %w_hbm.1, bf16[2,2,32,512]{3,2,1,0:T(8,128)(2,1)} %bitcast.1, bf16[256,256]{1,0:T(8,128)(2,1)} %constant.2.clone.had_hbm), custom_call_target="tpu_custom_call" | custom-call | tf_op jit(solution)/shard_map/rotated_projection/pallas_call | solution.py:414
  85.3 2.2 %place_results.1 = (bf16[128,512]{1,0:T(8,128)(2,1)}, bf16[32,2048]{1,0:T(8,128)(2,1)}, f32[2048,512]{1,0:T(8,128)}) custom-call(bf16[128,512]{1,0:T(8,128)(2,1)S(1)} %get-tuple-element.6.out_in, bf16[32,2048]{1,0:T(8,128)(2,1)S(1)} %get-tuple-element.7.ing_in, f32[2048,512]{1,0:T(8,128)S(1)} %get-tuple-element.8.wg_in), custom_call_target="tpu_custom_call" | custom-call | tf_op jit(solution)/shard_map/place_results/pallas_call | solution.py:448

commit v4 on v3

--- a/solution.py
+++ b/solution.py
@@ -11,7 +11,7 @@
 
 MESH = pl.DeviceIdType.MESH
 YL, Z, C, T, X = 2, 8, 2, 8, 4
-LO_CHUNKS = 4
+LO_CHUNKS = 5
 F32, BF16 = jnp.float32, jnp.bfloat16
 SEMS = 320
 
@@ -194,6 +194,7 @@
     arrive(r.at[block(1, z, c), lo], y_number)
     pass_on(1, pieces[1], z, 0)
     pass_on(-1, pieces[1], z, 0)
+    across(z, 0)
     share(1, z, lo)
 
     def ring_piece(s, piece):
@@ -205,31 +206,28 @@
             arrive(r.at[block(rel, zz, c), halves[half]], numbers[sign, piece, s])
             if s < 2 or (s == 2 and sign == far):
                 pass_on(sign, piece, zz, s + 1)
+            if rel == 0 and half == "hi":
+                across(zz, sign * (1 + s))
             share(rel, zz, halves[half])
 
     def ring_step(s):
         for piece in pieces:
             ring_piece(s, piece)
-
-    def across_send(s):
-        for sign in (1, -1):
-            if s < 3 or sign == 1:
-                across(z - sign * ahead * (1 + s), sign * (1 + s))
 
     def across_step(s):
         for sign in (1, -1):
             if s < 3 or sign == 1:
                 across_arrive(z - sign * ahead * (1 + s), sign * (1 + s))
 
-    ring_piece(0, pieces[0])
-    ring_piece(0, pieces[2])
+    ring_step(0)
     for j in range(1, X):
         from_x = (x + X - j) % X
         arrive(grad_rows(yh * X + from_x), near_numbers[j - 1])
         arrive(grad_rows((1 - yh) * X + from_x), far_numbers[j - 1])
     g2_number = pair()
     send(g.at[:, 1 - c], g2, sib, g2_number)
-    ring_piece(0, pieces[1])
+    across_arrive(z, 0)
+    ring_step(1)
     arrive(g2, g2_number)
     arrive(w2, w_number)
 
@@ -281,27 +279,18 @@
         for piece in order:
             reduce_piece(s, piece)
 
-    lax.fori_loop(lo_chunks, T, partial, 0)
-    for away in (4, 3, -3, 2, -2, 1, -1, 0):
-        give_across(away)
     lax.fori_loop(0, lo_chunks, partial, 0)
     reduce_piece(0, order[0])
     reduce_piece(0, order[1])
-    ring_step(1)
+    lax.fori_loop(lo_chunks, T, partial, 0)
+    across_step(0)
+    ring_step(2)
+    for away in (4, 3, -3, 2, -2, 1, -1, 0):
+        give_across(away)
+    across_step(1)
+    ring_step(3)
     reduce_piece(0, order[2])
-    across(z, 0)
-    across_send(0)
     reduce_step(1)
-    ring_step(2)
-    across_send(1)
-    across_send(2)
-    reduce_step(2)
-    ring_step(3)
-    across_send(3)
-    across_arrive(z, 0)
-    across_step(0)
-    reduce_step(3)
-    across_step(1)
     across_step(2)
 
     def products(i, carry):
@@ -328,7 +317,9 @@
     for j, peer in enumerate(along_x):
         send(q.at[:, (x + j + 1) % X], xq.at[x], peer, out_numbers[j])
     xq[x] = q[:, x]
+    reduce_step(2)
     lax.fori_loop(0, 3, weight_grad, 0)
+    reduce_step(3)
 
     def finals(piece):
         rel, half, far = piece
@@ -351,9 +342,6 @@
     for k, part in enumerate(local_rotation([rg[k] for k in range(T)])):
         t1[k] = part.astype(BF16)
     first_done = rotate_first(t1, v1)
-    lax.fori_loop(5, 8, weight_grad, 0)
-    first_done()
-    finish = rotate_second(v1, t2, igb)
 
     def out_sum(half):
         total = xq[0, half].astype(F32)
@@ -366,6 +354,9 @@
     os[...] = out_sum(1 - yh).astype(BF16)
     last_number = pair()
     send(os, oa, opposite, last_number)
+    first_done()
+    finish = rotate_second(v1, t2, igb)
+    lax.fori_loop(5, 8, weight_grad, 0)
     total = out_sum(yh)
     arrive(oa, last_number)
     out[...] = (total + oa[...].astype(F32)).astype(BF16)

time: 88 us -> 82.5 us (0.938)
  Pallas kernels: 86.9 us -> 81.7 us
    pallas_call x1, Pallas kernels: 84.7 us -> 79.6 us  [per_device(): pl.pallas_call(functools.partial(kernel, scale, grad_scale, LO_CHUNKS), o...]
where the time goes in v4:
time: 82.5 us; the launch traced here: 82.4 us
  Pallas kernels  81.7 us (99%)
    pallas_call x1, Pallas kernels, per_device(): pl.pallas_call(functools.partial(kernel, scale, grad_scale, LO_CHUNKS), o...  79.6 us
    pallas_call x1, Pallas kernels, per_device(): pl.pallas_call(place, out_shape=shapes, in_specs=[vmem] * 3, out_specs=(a...  2.18 us

profile of v4, /device:TPU:1, one launch (start us, length us, event | category | flops | bytes accessed | tf_op | source)
XLA Modules:
  0.0 82.4 jit_solution(6739089464313577148)
XLA Ops:
  0.6 79.6 %rotated_projection.1 = (bf16[128,512]{1,0:T(8,128)(2,1)S(1)}, bf16[32,2048]{1,0:T(8,128)(2,1)S(1)}, f32[2048,512]{1,0:T(8,128)S(1)}) custom-call(bf16[32,2048]{1,0:T(8,128)(2,1)} %act_hbm.1, bf16[2048,512]{1,0:T(8,128)(2,1)} %w_hbm.1, bf16[2,2,32,512]{3,2,1,0:T(8,128)(2,1)} %bitcast.1, bf16[256,256]{1,0:T(8,128)(2,1)} %constant.2.clone.had_hbm), custom_call_target="tpu_custom_call" | custom-call | tf_op jit(solution)/shard_map/rotated_projection/pallas_call | solution.py:405
  80.2 2.2 %place_results.1 = (bf16[128,512]{1,0:T(8,128)(2,1)}, bf16[32,2048]{1,0:T(8,128)(2,1)}, f32[2048,512]{1,0:T(8,128)}) custom-call(bf16[128,512]{1,0:T(8,128)(2,1)S(1)} %get-tuple-element.6.out_in, bf16[32,2048]{1,0:T(8,128)(2,1)S(1)} %get-tuple-element.7.ing_in, f32[2048,512]{1,0:T(8,128)S(1)} %get-tuple-element.8.wg_in), custom_call_target="tpu_custom_call" | custom-call | tf_op jit(solution)/shard_map/place_results/pallas_call | solution.py:439

commit v5 on v4

--- a/solution.py
+++ b/solution.py
@@ -11,7 +11,8 @@
 
 MESH = pl.DeviceIdType.MESH
 YL, Z, C, T, X = 2, 8, 2, 8, 4
-LO_CHUNKS = 5
+LO_CHUNKS = 4
+SUM_CHUNKS = 6
 F32, BF16 = jnp.float32, jnp.bfloat16
 SEMS = 320
 
@@ -37,7 +38,7 @@
     return parts
 
 
-def kernel(scale, grad_scale, lo_chunks, act_hbm, w_hbm, og_hbm, had_hbm, out, ing, wg, act, w, og, had,
+def kernel(scale, grad_scale, lo_chunks, sum_chunks, act_hbm, w_hbm, og_hbm, had_hbm, out, ing, wg, act, w, og, had,
            w2, s1, x1, s2, r, g, g2, pf, sbp, sbm, rp, rm, ybs, ybr, ys, yr, q, xq, os, oa, t1, v1, t2, igb,
            rg, sems, local_sems):
     d, t = lax.axis_index("dp"), lax.axis_index("tensor")
@@ -243,6 +244,8 @@
         pf[:, k] = total.reshape(Z * YL, tokens, chunk)
         return carry
 
+    sum_lo, sum_hi = pl.ds(0, sum_chunks), pl.ds(sum_chunks, T - sum_chunks)
+    sum_halves = {"lo": sum_lo, "hi": sum_hi}
     sums = {(sign, piece, s): pair() for sign in (1, -1) for piece in pieces for s in range(4)}
     back_numbers = {}
 
@@ -251,13 +254,13 @@
 
     def give_across(away):
         i = away + 4
-        ybs[i] = pf[target(1, z + ahead * away), hi].astype(BF16)
+        ybs[i] = pf[target(1, z + ahead * away), sum_hi].astype(BF16)
         back_numbers[away] = pair()
         send(ybs.at[i], ybr.at[i], yp, back_numbers[away])
 
     def reduce_piece(s, piece):
         rel, half, far = piece
-        part = halves[half]
+        part = sum_halves[half]
         for sign in (1, -1):
             if s == 0 and sign != far:
                 continue
@@ -279,12 +282,12 @@
         for piece in order:
             reduce_piece(s, piece)
 
-    lax.fori_loop(0, lo_chunks, partial, 0)
+    lax.fori_loop(0, sum_chunks, partial, 0)
     reduce_piece(0, order[0])
     reduce_piece(0, order[1])
-    lax.fori_loop(lo_chunks, T, partial, 0)
+    ring_step(2)
+    lax.fori_loop(sum_chunks, T, partial, 0)
     across_step(0)
-    ring_step(2)
     for away in (4, 3, -3, 2, -2, 1, -1, 0):
         give_across(away)
     across_step(1)
@@ -312,18 +315,19 @@
     across_step(3)
     for b, part, number in to_sib:
         arrive(r.at[b, part], number)
-    lax.fori_loop(0, 4, products, 0)
+    lax.fori_loop(0, 2, products, 0)
+    reduce_step(2)
+    lax.fori_loop(2, 4, products, 0)
     out_numbers = [pair() for _ in along_x]
     for j, peer in enumerate(along_x):
         send(q.at[:, (x + j + 1) % X], xq.at[x], peer, out_numbers[j])
     xq[x] = q[:, x]
-    reduce_step(2)
+    reduce_step(3)
     lax.fori_loop(0, 3, weight_grad, 0)
-    reduce_step(3)
 
     def finals(piece):
         rel, half, far = piece
-        part = halves[half]
+        part = sum_halves[half]
         total = pf[target(rel, z), part]
         for sign, into in ((1, rp), (-1, rm)):
             arrive(into.at[rel, 3, part], sums[sign, piece, 3])
@@ -333,12 +337,12 @@
     ys[...] = finals(order[0]).astype(BF16)
     back_number = pair()
     send(ys, yr, yp, back_number)
-    rg[lo] = finals(order[1])
+    rg[sum_lo] = finals(order[1])
     arrive(ybr.at[4], back_numbers[0])
-    rg[hi] = finals(order[2]) + ybr[4].astype(F32)
+    rg[sum_hi] = finals(order[2]) + ybr[4].astype(F32)
     lax.fori_loop(3, 5, weight_grad, 0)
     arrive(yr, back_number)
-    rg[lo] = rg[lo] + yr[...].astype(F32)
+    rg[sum_lo] = rg[sum_lo] + yr[...].astype(F32)
     for k, part in enumerate(local_rotation([rg[k] for k in range(T)])):
         t1[k] = part.astype(BF16)
     first_done = rotate_first(t1, v1)
@@ -395,15 +399,15 @@
     vmem = pl.BlockSpec(memory_space=pltpu.VMEM)
     anywhere = pl.BlockSpec(memory_space=pl.ANY)
     part = (T, tokens, chunk)
-    low = (LO_CHUNKS, tokens, chunk)
-    high = (T - LO_CHUNKS, tokens, chunk)
+    low = (SUM_CHUNKS, tokens, chunk)
+    high = (T - SUM_CHUNKS, tokens, chunk)
     shapes = (
         jax.ShapeDtypeStruct((out_grad.shape[0], features), BF16),
         jax.ShapeDtypeStruct((tokens, width), BF16),
         jax.ShapeDtypeStruct((width, features), F32),
     )
     results = pl.pallas_call(
-        functools.partial(kernel, scale, grad_scale, LO_CHUNKS),
+        functools.partial(kernel, scale, grad_scale, LO_CHUNKS, SUM_CHUNKS),
         out_shape=tuple(pltpu.VMEM(leaf.shape, leaf.dtype) for leaf in shapes),
         in_specs=[pl.BlockSpec(memory_space=pltpu.HBM)] * 4,
         out_specs=(vmem,) * 3,

time: 82.5 us -> 79 us (0.958)
  Pallas kernels: 81.7 us -> 78.3 us
    pallas_call x1, Pallas kernels: 79.6 us -> 76.1 us  [per_device(): pl.pallas_call(functools.partial(kernel, scale, grad_scale, LO_CHUNKS, SU...]
where the time goes in v5:
time: 79 us; the launch traced here: 78.9 us
  Pallas kernels  78.3 us (99%)
    pallas_call x1, Pallas kernels, per_device(): pl.pallas_call(functools.partial(kernel, scale, grad_scale, LO_CHUNKS, SU...  76.1 us
    pallas_call x1, Pallas kernels, per_device(): pl.pallas_call(place, out_shape=shapes, in_specs=[vmem] * 3, out_specs=(a...  2.18 us

profile of v5, /device:TPU:1, one launch (start us, length us, event | category | flops | bytes accessed | tf_op | source)
XLA Modules:
  0.0 78.9 jit_solution(8390763519381806779)
XLA Ops:
  0.6 76.1 %rotated_projection.1 = (bf16[128,512]{1,0:T(8,128)(2,1)S(1)}, bf16[32,2048]{1,0:T(8,128)(2,1)S(1)}, f32[2048,512]{1,0:T(8,128)S(1)}) custom-call(bf16[32,2048]{1,0:T(8,128)(2,1)} %act_hbm.1, bf16[2048,512]{1,0:T(8,128)(2,1)} %w_hbm.1, bf16[2,2,32,512]{3,2,1,0:T(8,128)(2,1)} %bitcast.1, bf16[256,256]{1,0:T(8,128)(2,1)} %constant.2.clone.had_hbm), custom_call_target="tpu_custom_call" | custom-call | tf_op jit(solution)/shard_map/rotated_projection/pallas_call | solution.py:409
  76.8 2.2 %place_results.1 = (bf16[128,512]{1,0:T(8,128)(2,1)}, bf16[32,2048]{1,0:T(8,128)(2,1)}, f32[2048,512]{1,0:T(8,128)}) custom-call(bf16[128,512]{1,0:T(8,128)(2,1)S(1)} %get-tuple-element.6.out_in, bf16[32,2048]{1,0:T(8,128)(2,1)S(1)} %get-tuple-element.7.ing_in, f32[2048,512]{1,0:T(8,128)S(1)} %get-tuple-element.8.wg_in), custom_call_target="tpu_custom_call" | custom-call | tf_op jit(solution)/shard_map/place_results/pallas_call | solution.py:443

commit v6 on v5

--- a/solution.py
+++ b/solution.py
@@ -12,7 +12,7 @@
 MESH = pl.DeviceIdType.MESH
 YL, Z, C, T, X = 2, 8, 2, 8, 4
 LO_CHUNKS = 4
-SUM_CHUNKS = 6
+SUM_CHUNKS = 7
 F32, BF16 = jnp.float32, jnp.bfloat16
 SEMS = 320
 

time: 79 us -> 79.6 us (level)
  no operation moved by 1% of the time
where the time goes in v6:
time: 79.6 us; the launch traced here: 79.5 us
  Pallas kernels  78.9 us (99%)
    pallas_call x1, Pallas kernels, per_device(): pl.pallas_call(functools.partial(kernel, scale, grad_scale, LO_CHUNKS, SU...  76.7 us
    pallas_call x1, Pallas kernels, per_device(): pl.pallas_call(place, out_shape=shapes, in_specs=[vmem] * 3, out_specs=(a...  2.18 us

profile of v6, /device:TPU:1, one launch (start us, length us, event | category | flops | bytes accessed | tf_op | source)
XLA Modules:
  0.0 79.5 jit_solution(1496050105071857021)
XLA Ops:
  0.6 76.7 %rotated_projection.1 = (bf16[128,512]{1,0:T(8,128)(2,1)S(1)}, bf16[32,2048]{1,0:T(8,128)(2,1)S(1)}, f32[2048,512]{1,0:T(8,128)S(1)}) custom-call(bf16[32,2048]{1,0:T(8,128)(2,1)} %act_hbm.1, bf16[2048,512]{1,0:T(8,128)(2,1)} %w_hbm.1, bf16[2,2,32,512]{3,2,1,0:T(8,128)(2,1)} %bitcast.1, bf16[256,256]{1,0:T(8,128)(2,1)} %constant.2.clone.had_hbm), custom_call_target="tpu_custom_call" | custom-call | tf_op jit(solution)/shard_map/rotated_projection/pallas_call | solution.py:409
  77.4 2.2 %place_results.1 = (bf16[128,512]{1,0:T(8,128)(2,1)}, bf16[32,2048]{1,0:T(8,128)(2,1)}, f32[2048,512]{1,0:T(8,128)}) custom-call(bf16[128,512]{1,0:T(8,128)(2,1)S(1)} %get-tuple-element.6.out_in, bf16[32,2048]{1,0:T(8,128)(2,1)S(1)} %get-tuple-element.7.ing_in, f32[2048,512]{1,0:T(8,128)S(1)} %get-tuple-element.8.wg_in), custom_call_target="tpu_custom_call" | custom-call | tf_op jit(solution)/shard_map/place_results/pallas_call | solution.py:443
